TPU v7x, 512 devices: a whole 4x4x16 slice. The times are simulated.
512 devices in a mesh: section: 2 (over core), dp: 64 (over z, y), mp: 4 (over x).
Axes of the slice: x: 4, y: 4, z: 16, core: 2. Of those that a mesh axis runs over, the one named last changes fastest.
Arguments:
- qkv: bfloat16 [8192, 3072], P('dp', ('section', 'mp')), may hold values from -6 to 6
- kv_cache: bfloat16 [4096, 8, 2048], P('dp', None, ('section', 'mp')), may hold values from -6 to 6
- residual: bfloat16 [8192, 2048], P('dp'), may hold values from -6 to 6
- out_weight: bfloat16 [1024, 2048], P(('section', 'mp')), may hold values from -0.1875 to 0.1875
- moe_gain: float32 [2048], replicated, may hold values from 0.1 to 1.9
- w_gate: bfloat16 [64, 2048, 1408], P('dp', None, ('section', 'mp')), may hold values from -0.125 to 0.125
- w_up: bfloat16 [64, 2048, 1408], P('dp', None, ('section', 'mp')), may hold values from -0.125 to 0.125
- w_down: bfloat16 [64, 1408, 2048], P('dp', ('section', 'mp')), may hold values from -0.15625 to 0.15625
- seg_ids: int32 [64, 1, 128], P('dp'), may hold values from 0 to 3, never falling along the last dimension, each value on 1 to 64 neighbouring positions
- prefix_blocks: int32 [64, 1, 4], P('dp'), may hold values from 1 to 32, 64 in all within a row
- owners: int32 [64, 1, 64, 1], replicated, may hold values from 0 to 63; in each aligned block of 64 rows (0 to 63, 64 to 127, ..., all dimensions but the last counted through in order) at most 3 rows name the same one
- slot_ids: int32 [64, 1, 64], replicated, may hold values from 0 to 63
- expert_ids: int32 [8192, 4], P('dp'), may hold values from 0 to 63, all different within a row; in each aligned block of 16 rows (0 to 15, 16 to 31, ...) at most 2 rows name the same one
- gate_weights: float32 [8192, 4], P('dp'), may hold values from 0.05 to 0.5
Outputs:
- layer_out: bfloat16 [8192, 2048], P('dp', ('section', 'mp'))
Inputs may be any that keep to these rules, and one draw needn't show every extreme that they name: seg_ids[g, m] never falls along the tokens; each of the 4 requests has 1 to 64 tokens, one exactly 64. `prefix_blocks`: the 4 counts of each (g, m) sum to 64, one of them is 32. `owners`: in each block table of 64 entries no owner appears more than 3 times, and some owner appears exactly 3 times in some table. `expert_ids`: each token names 4 different experts; in each aligned block of 16 tokens no expert is named by more than 2 tokens, a bound that some block reaches.
All inputs are finite; a program needn't handle non-finite values.
Results may differ from a plain program's by a relative error of at most 0.009.
Values may be sent and summed in bfloat16 or wider, within the bound.
No kernel may reach another device: no remote copies, remote signals or barrier semaphores. Data moves between devices by JAX's collectives and lax.ppermute only.
A program may use at most 64 MiB of HBM per device.

v0:
```python
import math
import jax
import jax.numpy as jnp
from jax import lax
from jax.sharding import PartitionSpec as P

HEAD_DIM = 128
TOPK = 4
PREF = 64
BLK = 8


def normalize(hidden, gain):
    square = jnp.mean(hidden * hidden, axis=-1, keepdims=True)
    return (hidden * lax.rsqrt(square + 1e-06) * gain).astype(jnp.bfloat16)


def expert_rows(inputs, w_gate, w_up, w_down):
    model_width = inputs.shape[-1]
    flat_rows = inputs.reshape(-1, model_width)
    gate_rows = jnp.dot(flat_rows, w_gate[0], preferred_element_type=jnp.float32)
    up_rows = jnp.dot(flat_rows, w_up[0], preferred_element_type=jnp.float32)
    hidden = (jax.nn.silu(gate_rows) * up_rows).astype(jnp.bfloat16)
    result = jnp.dot(hidden, w_down[0], preferred_element_type=jnp.float32).astype(jnp.bfloat16)
    return result.reshape(inputs.shape[:-1] + (result.shape[-1],))


def slot_table(pair_ids, pair_slots, experts, capacity):
    pair_count = pair_ids.shape[0]
    expert_match = pair_ids[None, None, :] == jnp.arange(experts, dtype=jnp.int32)[:, None, None]
    slot_match = pair_slots[None, None, :] == jnp.arange(capacity, dtype=jnp.int32)[None, :, None]
    pair_match = expert_match & slot_match
    token_of = jnp.arange(pair_count, dtype=jnp.int32) // TOPK
    source = jnp.sum(jnp.where(pair_match, token_of[None, None, :], 0), axis=2)
    filled = jnp.any(pair_match, axis=2)
    return (source, filled)


def dispatch_rows(normed, source, filled):
    gathered = jnp.take(normed, source.reshape(-1), axis=0).reshape(
        source.shape + (normed.shape[-1],)
    )
    return jnp.where(filled[:, :, None], gathered, jnp.zeros_like(gathered))


def local(
    qkv,
    kv_cache,
    residual,
    out_weight,
    moe_gain,
    w_gate,
    w_up,
    w_down,
    seg_ids,
    prefix_blocks,
    owners,
    slot_ids,
    expert_ids,
    gate_weights,
):
    groups = lax.axis_size("dp")
    shards = lax.axis_size("section") * lax.axis_size("mp")
    group_index = lax.axis_index("dp")
    shard_index = lax.axis_index("section") * lax.axis_size("mp") + lax.axis_index("mp")
    mb_rows = seg_ids.shape[2]
    quarter_rows = mb_rows // shards
    model_width = residual.shape[1]
    part_cols = model_width // shards
    head_cols = out_weight.shape[0]
    heads_local = head_cols // HEAD_DIM
    cache_cols = kv_cache.shape[2]
    quarter_cap = min(quarter_rows, max(2, 2 * quarter_rows * TOPK // groups))
    capacity = shards * quarter_cap
    owner_cap = max(3, 3 * PREF // groups)
    score_scale = 1.0 / math.sqrt(HEAD_DIM)
    own_table = owners[:, 0, :, 0]
    slot_table_m = slot_ids[:, 0, :]
    owned_here = own_table == group_index
    local_order = jnp.cumsum(owned_here.astype(jnp.int32), axis=1) - 1
    wanted = owned_here[:, None, :] & (
        local_order[:, None, :] == jnp.arange(owner_cap, dtype=jnp.int32)[None, :, None]
    )
    slot_pick = jnp.sum(jnp.where(wanted, slot_table_m[:, None, :], 0), axis=2)
    filled = jnp.any(wanted, axis=2)
    chosen = jnp.take(kv_cache, slot_pick.reshape(-1), axis=0).reshape(
        groups, owner_cap, BLK, cache_cols
    )
    chosen = jnp.where(filled[:, :, None, None], chosen, jnp.zeros_like(chosen))
    arrived = lax.all_to_all(chosen, "dp", split_axis=0, concat_axis=0, tiled=True)
    my_owner = lax.dynamic_index_in_dim(own_table, group_index, 0, keepdims=False)
    block_index = jnp.arange(PREF, dtype=jnp.int32)
    earlier = (my_owner[None, :] == my_owner[:, None]) & (
        block_index[None, :] < block_index[:, None]
    )
    my_rank = jnp.sum(earlier.astype(jnp.int32), axis=1)
    where_from = my_owner * owner_cap + my_rank
    prefix = jnp.take(arrived.reshape(groups * owner_cap, BLK, cache_cols), where_from, axis=0)
    prefix = prefix.reshape(PREF * BLK, heads_local, 2, HEAD_DIM)
    tokens = qkv
    tokens = tokens.reshape(mb_rows, heads_local, 3, HEAD_DIM)
    query_rows = tokens[:, :, 0]
    key_rows = jnp.concatenate([prefix[:, :, 0], tokens[:, :, 1]], axis=0)
    value_rows = jnp.concatenate([prefix[:, :, 1], tokens[:, :, 2]], axis=0)
    segments = seg_ids[0, 0]
    block_ends = jnp.cumsum(prefix_blocks[0, 0])
    block_seg = jnp.sum((block_ends[None, :] <= block_index[:, None]).astype(jnp.int32), axis=1)
    prefix_seg = jnp.repeat(block_seg, BLK)
    position = jnp.arange(mb_rows, dtype=jnp.int32)
    same_prefix = prefix_seg[None, :] == segments[:, None]
    same_new = (segments[None, :] == segments[:, None]) & (position[None, :] <= position[:, None])
    visible = jnp.concatenate([same_prefix, same_new], axis=1)
    scores = (
        jnp.einsum("qhd,khd->hqk", query_rows, key_rows, preferred_element_type=jnp.float32)
        * score_scale
    )
    scores = jnp.where(visible[None], scores, -jnp.inf)
    row_max = jnp.max(scores, axis=2, keepdims=True)
    weights = jnp.exp(scores - row_max)
    attention = (weights / jnp.sum(weights, axis=2, keepdims=True)).astype(jnp.bfloat16)
    combined = jnp.einsum("hqk,khd->qhd", attention, value_rows, preferred_element_type=jnp.float32)
    attended_now = combined.astype(jnp.bfloat16).reshape(mb_rows, head_cols)
    stream = residual.astype(jnp.float32)
    projected = jnp.dot(attended_now, out_weight, preferred_element_type=jnp.float32)
    quarter_ids = expert_ids.reshape(shards, quarter_rows * TOPK)
    one_hot = (
        quarter_ids[:, :, None] == jnp.arange(groups, dtype=jnp.int32)[None, None, :]
    ).astype(jnp.int32)
    quarter_rank = jnp.sum((jnp.cumsum(one_hot, axis=1) - one_hot) * one_hot, axis=2)
    flat_ids = expert_ids.reshape(-1)
    flat_slot = (quarter_rank + jnp.arange(shards, dtype=jnp.int32)[:, None] * quarter_cap).reshape(
        -1
    )
    mixed_in = stream + lax.psum(projected, ("section", "mp"))
    normed = normalize(mixed_in, moe_gain)
    source, filled = slot_table(flat_ids, flat_slot, groups, capacity)
    outgoing = dispatch_rows(normed, source, filled)
    incoming = lax.all_to_all(outgoing, "dp", split_axis=0, concat_axis=0, tiled=True)
    produced = expert_rows(incoming, w_gate, w_up, w_down)
    returned = lax.all_to_all(produced, "dp", split_axis=0, concat_axis=0, tiled=True)
    position = flat_ids * capacity + flat_slot
    picked = jnp.take(returned.reshape(groups * capacity, model_width), position, axis=0)
    picked = picked.reshape(mb_rows, TOPK, model_width)
    weighted = jnp.einsum("tk,tkd->td", gate_weights, picked.astype(jnp.float32))
    moe_full = lax.psum(weighted.astype(jnp.bfloat16), ("section", "mp")).astype(jnp.float32)
    finished = (mixed_in + moe_full).astype(jnp.bfloat16).reshape(mb_rows, shards, part_cols)
    return lax.dynamic_index_in_dim(finished, shard_index, 1, keepdims=False)


def solution(mesh):
    return jax.shard_map(
        local,
        mesh=mesh,
        in_specs=(
            P("dp", ("section", "mp")),
            P("dp", None, ("section", "mp")),
            P("dp", None),
            P(("section", "mp"), None),
            P(),
            P("dp", None, ("section", "mp")),
            P("dp", None, ("section", "mp")),
            P("dp", ("section", "mp"), None),
            P("dp", None, None),
            P("dp", None, None),
            P(),
            P(),
            P("dp", None),
            P("dp", None),
        ),
        out_specs=P("dp", ("section", "mp")),
        check_vma=False,
    )
```

profile of v0, /device:TPU:8, one launch (start us, length us, event | category | flops | bytes accessed | tf_op | source)
XLA Modules:
  0.0 661.5 jit_solution(7814979342064895918)
XLA Ops:
  6.6 0.9 broadcast_compare_fusion.1
  7.7 0.9 select_reduce_fusion
  9.2 1.8 gather_fusion
  11.0 1.3 select_select_fusion.1
  12.4 18.7 %all-to-all-start = ((bf16[64,3,8,256]{3,2,1,0:T(8,128)(2,1)}), bf16[64,3,8,256]{3,2,1,0:T(8,128)(2,1)S(1)}, u32[]{:S(2)}, u32[]{:S(2)}) async-start(bf16[64,3,8,256]{3,2,1,0:T(8,128)(2,1)} %select_select_fusion.1), calls=%async_computation | async-start | bytes 1572864 | tf_op jit(solution)/shard_map/all_to_all | solution.py:90
  31.5 0.7 fusion.43
  32.3 0.7 compare_and_fusion.3
  34.1 1.4 fusion.53
  35.7 1.2 fusion
  37.0 0.7 fusion.42
  37.9 37.1 %all-to-all-done = bf16[64,3,8,256]{3,2,1,0:T(8,128)(2,1)S(1)} async-done(((bf16[64,3,8,256]{3,2,1,0:T(8,128)(2,1)}), bf16[64,3,8,256]{3,2,1,0:T(8,128)(2,1)S(1)}, u32[]{:S(2)}, u32[]{:S(2)}) %all-to-all-start) | async-done | bytes 786464 | tf_op jit(solution)/shard_map/all_to_all | solution.py:90
  75.7 1.8 broadcast_select_fusion
  78.3 1.5 fusion.8
  79.8 1.2 and_reduce_fusion
  81.0 68.3 %all-reduce.3.cloned.1.call-done = f32[128,2048]{1,0:T(8,128)} async-done(((f32[128,2048]{1,0:T(8,128)}), f32[128,2048]{1,0:T(8,128)}) %all-reduce.3.cloned.1.call-update) | async-done | bytes 1048592 | tf_op jit(solution)/shard_map/psum | solution.py:134
  149.4 1.4 multiply_reduce_fusion
  150.8 1.4 multiply_convert_fusion
  152.2 6.0 gather_fusion.2
  158.3 2.6 select_select_fusion
  160.8 203.6 %all_to_all.15 = bf16[64,16,2048]{2,1,0:T(8,128)(2,1)S(1)} all-to-all(bf16[64,16,2048]{2,1,0:T(8,128)(2,1)S(1)} %select_select_fusion), channel_id=1, replica_groups=mesh['section'=2,'dp'=64,'mp'=4] {'dp'}, dimensions={0} | all-to-all | bytes 8388608 | tf_op jit(solution)/shard_map/all_to_all | solution.py:138
  364.5 2.0 copy-done.3
  366.5 1.5 fusion.14
  368.0 6.8 %convolution_convert_fusion = bf16[1024,2048]{1,0:T(8,128)(2,1)} fusion(bf16[1024,2048]{1,0:T(8,128)(2,1)} %bitcast.88, bf16[1,176,2048]{2,1,0:T(8,128)(2,1)S(1)} %copy-done, bf16[1,2048,176]{1,2,0:T(8,128)(2,1)S(1)} %copy-done.11, f32[1024,176]{0,1:T(8,128)S(1)} %fusion.14), kind=kOutput, calls=%fused_computation.5 | convolution fusion | flops 1479573504 | bytes 10551296 | tf_op jit(solution)/shard_map/dot_general | solution.py:24
  374.9 6.3 all-to-all-start.2
  382.2 186.9 %all-to-all-done.2 = bf16[64,16,2048]{2,1,0:T(8,128)(2,1)} async-done(((bf16[64,16,2048]{2,1,0:T(8,128)(2,1)}), bf16[64,16,2048]{2,1,0:T(8,128)(2,1)}, u32[]{:S(2)}, u32[]{:S(2)}) %all-to-all-start.2) | async-done | bytes 4194336 | tf_op jit(solution)/shard_map/all_to_all | solution.py:140
  569.1 7.1 %gather_fusion.3 = bf16[512,2048]{1,0:T(8,128)(2,1)S(1)} fusion(bf16[1024,2048]{1,0:T(8,128)(2,1)} %bitcast.28, s32[1024]{0:T(1024)S(1)} %pad_clamp_fusion), kind=kCustom, calls=%fused_computation.3 | custom fusion | bytes 4196352 | tf_op jit(solution)/shard_map/jit(_take)/gather | solution.py:142
  576.2 2.2 gather.31
  578.5 3.0 fusion.1
  581.5 1.1 copy.100
  582.6 69.9 %all-reduce.5.cloned.1.call-done = bf16[128,2048]{1,0:T(8,128)(2,1)} async-done(((bf16[128,2048]{1,0:T(8,128)(2,1)}), bf16[128,2048]{1,0:T(8,128)(2,1)}) %all-reduce.5.cloned.1.call-update) | async-done | bytes 524304 | tf_op jit(solution)/shard_map/psum | solution.py:145
  652.5 1.2 add_convert_fusion
  654.0 0.6 copy.101
  (91 shorter events, 5.8 us)
Async XLA Ops:
  6.5 361.5 %copy-start = (bf16[1,176,2048]{2,1,0:T(8,128)(2,1)S(1)}, bf16[1,176,2048]{2,1,0:T(8,128)(2,1)}, u32[]{:S(2)}) copy-start(bf16[1,176,2048]{2,1,0:T(8,128)(2,1)} %param.21) | copy-start | bytes 2162692
  6.5 24.6 %copy-start.6 = (s32[128,4]{0,1:T(4,128)S(1)}, s32[128,4]{0,1:T(4,128)}, u32[]{:S(2)}) copy-start(s32[128,4]{0,1:T(4,128)} %param.26) | copy-start | bytes 6148
  6.5 26.6 %copy-start.5 = (bf16[128,384]{1,0:T(8,128)(2,1)S(1)}, bf16[128,384]{1,0:T(8,128)(2,1)}, u32[]{:S(2)}) copy-start(bf16[128,384]{1,0:T(8,128)(2,1)} %param.14) | copy-start | bytes 294916
  6.5 26.9 %copy-start.12 = (s32[1,1,4]{2,1,0:T(1,128)S(1)}, s32[1,1,4]{2,1,0:T(1,128)}, u32[]{:S(2)}) copy-start(s32[1,1,4]{2,1,0:T(1,128)} %param.23) | copy-start | bytes 52
  6.5 31.1 %copy-start.8 = (s32[1,1,128]{2,1,0:T(1,128)S(1)}, s32[1,1,128]{2,1,0:T(1,128)}, u32[]{:S(2)}) copy-start(s32[1,1,128]{2,1,0:T(1,128)} %param.22) | copy-start | bytes 1540
  11.0 67.2 %copy-start.4 = (bf16[128,2048]{1,0:T(8,128)(2,1)S(1)}, bf16[128,2048]{1,0:T(8,128)(2,1)}, u32[]{:S(2)}) copy-start(bf16[128,2048]{1,0:T(8,128)(2,1)} %param.17) | copy-start | bytes 1572868
  12.4 62.7 %all-to-all-start = ((bf16[64,3,8,256]{3,2,1,0:T(8,128)(2,1)}), bf16[64,3,8,256]{3,2,1,0:T(8,128)(2,1)S(1)}, u32[]{:S(2)}, u32[]{:S(2)}) async-start(bf16[64,3,8,256]{3,2,1,0:T(8,128)(2,1)} %select_select_fusion.1), calls=%async_computation | async-start | bytes 1572864 | tf_op jit(solution)/shard_map/all_to_all | solution.py:90
  31.1 118.3 %all-reduce.3.cloned.1.call-start = ((), (), s32[]{:S(2)}) async-start(), calls=%async_computation.3 | async-start | bytes 2097152 | tf_op jit(solution)/shard_map/psum | solution.py:134
  33.8 115.6 %copy-start.2 = (bf16[128,2048]{1,0:T(8,128)(2,1)S(1)}, bf16[128,2048]{1,0:T(8,128)(2,1)}, u32[]{:S(2)}) copy-start(bf16[128,2048]{1,0:T(8,128)(2,1)} %param.16) | copy-start | bytes 1572868
  75.7 75.1 %copy-start.7 = (f32[2048]{0:T(1024)S(1)}, f32[2048]{0:T(1024)}, u32[]{:S(2)}) copy-start(f32[2048]{0:T(1024)} %param.18) | copy-start | bytes 24580
  160.8 205.6 %copy-start.10 = (bf16[1,2048,176]{1,2,0:T(8,128)(2,1)S(1)}, bf16[1,2048,176]{1,2,0:T(8,128)(2,1)}, u32[]{:S(2)}) copy-start(bf16[1,2048,176]{1,2,0:T(8,128)(2,1)} %param.19) | copy-start | bytes 2162692
  364.5 2.0 copy-start.3
  364.5 3.5 copy-start.11
  374.9 7.1 %copy-start.9 = (f32[128,4]{0,1:T(4,128)S(1)}, f32[128,4]{0,1:T(4,128)}, u32[]{:S(2)}) copy-start(f32[128,4]{0,1:T(4,128)} %param.27) | copy-start | bytes 6148
  374.9 194.2 %all-to-all-start.2 = ((bf16[64,16,2048]{2,1,0:T(8,128)(2,1)}), bf16[64,16,2048]{2,1,0:T(8,128)(2,1)}, u32[]{:S(2)}, u32[]{:S(2)}) async-start(bf16[64,16,2048]{2,1,0:T(8,128)(2,1)} %bitcast.86), calls=%async_computation.2 | async-start | bytes 8388608 | tf_op jit(solution)/shard_map/all_to_all | solution.py:140
  381.2 271.3 %all-reduce.5.cloned.1.call-start = ((), (), s32[]{:S(2)}) async-start(), calls=%async_computation.4 | async-start | bytes 1048576 | tf_op jit(solution)/shard_map/psum | solution.py:145
  578.5 74.0 %copy-start.1 = (f32[128,2048]{1,0:T(8,128)S(1)}, f32[128,2048]{1,0:T(8,128)}, u32[]{:S(2)}) copy-start(f32[128,2048]{1,0:T(8,128)} %all-reduce.3.cloned.1.call-done) | copy-start | bytes 3145732
Sparse Core Ops, SparseCore 0:
  79.9 69.3 all-reduce.2
  582.8 69.7 all-reduce.4
where the time goes:
time: 662 us; the launch traced here: 661 us
  waiting for transfers between devices  362 us (55%)
  blocking collectives  204 us (31%)
  local copies, waits for them, and re-layouts  25.6 us (4%)
  starting transfers between devices  25.1 us (4%)
  other arithmetic  17.9 us (3%)
  between operations  13.8 us (2%)
  matrix products  13.2 us (2%)
    all_to_all x1, blocking collectives, local(): lax.all_to_all(outgoing, 'dp', split_axis=0, concat_axis=0, tiled=True)  204 us
    all_to_all x1, waiting for transfers between devices, local(): lax.all_to_all(produced, 'dp', split_axis=0, concat_axis=0, tiled=True)  187 us
    psum x1, waiting for transfers between devices, local(): lax.psum(weighted.astype(jnp.bfloat16), ('section', 'mp'))  69.9 us
    psum x1, waiting for transfers between devices, local(): mixed_in = stream + lax.psum(projected, ('section', 'mp'))  68.3 us
    all_to_all x1, waiting for transfers between devices, local(): lax.all_to_all(chosen, 'dp', split_axis=0, concat_axis=0, tiled=True)  37.1 us
    all_to_all x1, starting transfers between devices, local(): lax.all_to_all(chosen, 'dp', split_axis=0, concat_axis=0, tiled=True)  18.7 us
  transfers between devices with their start and end apart: 4, of which 4 were waited for; matrix products, arithmetic and copies ran while one was open for 1% of the time, Pallas kernels for 0%

commit v1 on v0

--- a/solution.py
+++ b/solution.py
@@ -142,7 +142,9 @@
     picked = jnp.take(returned.reshape(groups * capacity, model_width), position, axis=0)
     picked = picked.reshape(mb_rows, TOPK, model_width)
     weighted = jnp.einsum("tk,tkd->td", gate_weights, picked.astype(jnp.float32))
-    moe_full = lax.psum(weighted.astype(jnp.bfloat16), ("section", "mp")).astype(jnp.float32)
+    moe_full = jnp.sum(
+        lax.all_gather(weighted.astype(jnp.bfloat16), ("section", "mp")), axis=0
+    ).astype(jnp.float32)
     finished = (mixed_in + moe_full).astype(jnp.bfloat16).reshape(mb_rows, shards, part_cols)
     return lax.dynamic_index_in_dim(finished, shard_index, 1, keepdims=False)
 

time: 662 us -> 629 us (0.950)
  the two profiles are of different devices: /device:TPU:8 before, /device:TPU:1 now
where the time goes in v1:
time: 629 us; the launch traced here: 628 us
  waiting for transfers between devices  327 us (52%)
  blocking collectives  199 us (32%)
  starting transfers between devices  29.7 us (5%)
  local copies, waits for them, and re-layouts  25.5 us (4%)
  other arithmetic  19.9 us (3%)
  between operations  13.9 us (2%)
  matrix products  13.1 us (2%)
    all_to_all x1, blocking collectives, local(): lax.all_to_all(outgoing, 'dp', split_axis=0, concat_axis=0, tiled=True)  199 us
    all_to_all x1, waiting for transfers between devices, local(): lax.all_to_all(produced, 'dp', split_axis=0, concat_axis=0, tiled=True)  181 us
    psum x1, waiting for transfers between devices, local(): mixed_in = stream + lax.psum(projected, ('section', 'mp'))  70.4 us
    all_gather x1, waiting for transfers between devices, local(): lax.all_gather(weighted.astype(jnp.bfloat16), ('section', 'mp'))  41.8 us
    all_to_all x1, waiting for transfers between devices, local(): lax.all_to_all(chosen, 'dp', split_axis=0, concat_axis=0, tiled=True)  33.9 us
    all_to_all x1, starting transfers between devices, local(): lax.all_to_all(chosen, 'dp', split_axis=0, concat_axis=0, tiled=True)  19.3 us
  transfers between devices with their start and end apart: 4, of which 4 were waited for; matrix products, arithmetic and copies ran while one was open for 1% of the time, Pallas kernels for 0%

profile of v1, /device:TPU:1, one launch (start us, length us, event | category | flops | bytes accessed | tf_op | source)
XLA Modules:
  0.0 628.4 jit_solution(12480277132106734808)
XLA Ops:
  6.6 0.9 broadcast_compare_fusion.1
  7.7 0.9 select_reduce_fusion
  9.2 1.8 gather_fusion
  11.0 1.3 select_select_fusion.1
  12.4 19.3 %all-to-all-start = ((bf16[64,3,8,256]{3,2,1,0:T(8,128)(2,1)}), bf16[64,3,8,256]{3,2,1,0:T(8,128)(2,1)S(1)}, u32[]{:S(2)}, u32[]{:S(2)}) async-start(bf16[64,3,8,256]{3,2,1,0:T(8,128)(2,1)} %select_select_fusion.1), calls=%async_computation | async-start | bytes 1572864 | tf_op jit(solution)/shard_map/all_to_all | solution.py:90
  32.0 0.7 fusion.43
  32.9 0.7 compare_and_fusion.3
  34.6 1.4 fusion.53
  36.3 1.2 fusion
  37.6 0.7 fusion.42
  38.5 33.9 %all-to-all-done = bf16[64,3,8,256]{3,2,1,0:T(8,128)(2,1)S(1)} async-done(((bf16[64,3,8,256]{3,2,1,0:T(8,128)(2,1)}), bf16[64,3,8,256]{3,2,1,0:T(8,128)(2,1)S(1)}, u32[]{:S(2)}, u32[]{:S(2)}) %all-to-all-start) | async-done | bytes 786464 | tf_op jit(solution)/shard_map/all_to_all | solution.py:90
  73.0 1.8 broadcast_select_fusion
  75.6 1.5 fusion.8
  77.1 1.2 and_reduce_fusion
  78.3 70.4 %all-reduce.2.cloned.1.call-done = f32[128,2048]{1,0:T(8,128)} async-done(((f32[128,2048]{1,0:T(8,128)}), f32[128,2048]{1,0:T(8,128)}) %all-reduce.2.cloned.1.call-update) | async-done | bytes 1048592 | tf_op jit(solution)/shard_map/psum | solution.py:134
  148.7 1.4 multiply_reduce_fusion
  150.2 1.4 multiply_convert_fusion
  151.6 6.0 gather_fusion.2
  157.6 2.6 select_select_fusion
  160.2 198.9 %all_to_all.15 = bf16[64,16,2048]{2,1,0:T(8,128)(2,1)S(1)} all-to-all(bf16[64,16,2048]{2,1,0:T(8,128)(2,1)S(1)} %select_select_fusion), channel_id=1, replica_groups=mesh['section'=2,'dp'=64,'mp'=4] {'dp'}, dimensions={0} | all-to-all | bytes 8388608 | tf_op jit(solution)/shard_map/all_to_all | solution.py:138
  359.1 2.0 copy-done.3
  361.1 1.5 fusion.14
  362.6 6.8 %convolution_convert_fusion = bf16[1024,2048]{1,0:T(8,128)(2,1)} fusion(bf16[1024,2048]{1,0:T(8,128)(2,1)} %bitcast.90, bf16[1,176,2048]{2,1,0:T(8,128)(2,1)S(1)} %copy-done, bf16[1,2048,176]{1,2,0:T(8,128)(2,1)S(1)} %copy-done.11, f32[1024,176]{0,1:T(8,128)S(1)} %fusion.14), kind=kOutput, calls=%fused_computation.5 | convolution fusion | flops 1479573504 | bytes 10551296 | tf_op jit(solution)/shard_map/dot_general | solution.py:24
  369.5 10.3 %all-to-all-start.2 = ((bf16[64,16,2048]{2,1,0:T(8,128)(2,1)}), bf16[64,16,2048]{2,1,0:T(8,128)(2,1)}, u32[]{:S(2)}, u32[]{:S(2)}) async-start(bf16[64,16,2048]{2,1,0:T(8,128)(2,1)} %bitcast.88), calls=%async_computation.2 | async-start | bytes 8388608 | tf_op jit(solution)/shard_map/all_to_all | solution.py:140
  380.9 181.4 %all-to-all-done.2 = bf16[64,16,2048]{2,1,0:T(8,128)(2,1)} async-done(((bf16[64,16,2048]{2,1,0:T(8,128)(2,1)}), bf16[64,16,2048]{2,1,0:T(8,128)(2,1)}, u32[]{:S(2)}, u32[]{:S(2)}) %all-to-all-start.2) | async-done | bytes 4194336 | tf_op jit(solution)/shard_map/all_to_all | solution.py:140
  562.2 7.1 %gather_fusion.3 = bf16[512,2048]{1,0:T(8,128)(2,1)S(1)} fusion(bf16[1024,2048]{1,0:T(8,128)(2,1)} %bitcast.28, s32[1024]{0:T(1024)S(1)} %pad_clamp_fusion), kind=kCustom, calls=%fused_computation.3 | custom fusion | bytes 4196352 | tf_op jit(solution)/shard_map/jit(_take)/gather | solution.py:142
  569.4 2.2 gather.31
  571.6 2.9 fusion.1
  574.5 1.1 copy.100
  575.7 41.8 %all-gather.3.cloned.1.call-done = bf16[1024,2048]{1,0:T(8,128)(2,1)} async-done(((bf16[128,2048]{1,0:T(8,128)(2,1)}), bf16[1024,2048]{1,0:T(8,128)(2,1)}) %all-gather.3.cloned.1.call-update) | async-done | bytes 4194320 | tf_op jit(solution)/shard_map/all_gather | solution.py:146
  617.5 3.0 reduce_sum.88
  620.9 0.6 copy.101
  (92 shorter events, 6.0 us)
Async XLA Ops:
  6.5 356.1 %copy-start = (bf16[1,176,2048]{2,1,0:T(8,128)(2,1)S(1)}, bf16[1,176,2048]{2,1,0:T(8,128)(2,1)}, u32[]{:S(2)}) copy-start(bf16[1,176,2048]{2,1,0:T(8,128)(2,1)} %param.21) | copy-start | bytes 2162692
  6.5 25.2 %copy-start.6 = (s32[128,4]{0,1:T(4,128)S(1)}, s32[128,4]{0,1:T(4,128)}, u32[]{:S(2)}) copy-start(s32[128,4]{0,1:T(4,128)} %param.26) | copy-start | bytes 6148
  6.5 27.2 %copy-start.5 = (bf16[128,384]{1,0:T(8,128)(2,1)S(1)}, bf16[128,384]{1,0:T(8,128)(2,1)}, u32[]{:S(2)}) copy-start(bf16[128,384]{1,0:T(8,128)(2,1)} %param.14) | copy-start | bytes 294916
  6.5 27.4 %copy-start.12 = (s32[1,1,4]{2,1,0:T(1,128)S(1)}, s32[1,1,4]{2,1,0:T(1,128)}, u32[]{:S(2)}) copy-start(s32[1,1,4]{2,1,0:T(1,128)} %param.23) | copy-start | bytes 52
  6.5 31.7 %copy-start.8 = (s32[1,1,128]{2,1,0:T(1,128)S(1)}, s32[1,1,128]{2,1,0:T(1,128)}, u32[]{:S(2)}) copy-start(s32[1,1,128]{2,1,0:T(1,128)} %param.22) | copy-start | bytes 1540
  11.0 64.5 %copy-start.4 = (bf16[128,2048]{1,0:T(8,128)(2,1)S(1)}, bf16[128,2048]{1,0:T(8,128)(2,1)}, u32[]{:S(2)}) copy-start(bf16[128,2048]{1,0:T(8,128)(2,1)} %param.17) | copy-start | bytes 1572868
  12.4 60.0 %all-to-all-start = ((bf16[64,3,8,256]{3,2,1,0:T(8,128)(2,1)}), bf16[64,3,8,256]{3,2,1,0:T(8,128)(2,1)S(1)}, u32[]{:S(2)}, u32[]{:S(2)}) async-start(bf16[64,3,8,256]{3,2,1,0:T(8,128)(2,1)} %select_select_fusion.1), calls=%async_computation | async-start | bytes 1572864 | tf_op jit(solution)/shard_map/all_to_all | solution.py:90
  31.6 117.1 %all-reduce.2.cloned.1.call-start = ((), (), s32[]{:S(2)}) async-start(), calls=%async_computation.3 | async-start | bytes 2097152 | tf_op jit(solution)/shard_map/psum | solution.py:134
  34.3 114.4 %copy-start.2 = (bf16[128,2048]{1,0:T(8,128)(2,1)S(1)}, bf16[128,2048]{1,0:T(8,128)(2,1)}, u32[]{:S(2)}) copy-start(bf16[128,2048]{1,0:T(8,128)(2,1)} %param.16) | copy-start | bytes 1572868
  73.0 77.2 %copy-start.7 = (f32[2048]{0:T(1024)S(1)}, f32[2048]{0:T(1024)}, u32[]{:S(2)}) copy-start(f32[2048]{0:T(1024)} %param.18) | copy-start | bytes 24580
  160.2 200.9 %copy-start.10 = (bf16[1,2048,176]{1,2,0:T(8,128)(2,1)S(1)}, bf16[1,2048,176]{1,2,0:T(8,128)(2,1)}, u32[]{:S(2)}) copy-start(bf16[1,2048,176]{1,2,0:T(8,128)(2,1)} %param.19) | copy-start | bytes 2162692
  359.1 2.0 copy-start.3
  359.1 3.5 copy-start.11
  369.5 11.2 %copy-start.9 = (f32[128,4]{0,1:T(4,128)S(1)}, f32[128,4]{0,1:T(4,128)}, u32[]{:S(2)}) copy-start(f32[128,4]{0,1:T(4,128)} %param.27) | copy-start | bytes 6148
  369.5 192.8 %all-to-all-start.2 = ((bf16[64,16,2048]{2,1,0:T(8,128)(2,1)}), bf16[64,16,2048]{2,1,0:T(8,128)(2,1)}, u32[]{:S(2)}, u32[]{:S(2)}) async-start(bf16[64,16,2048]{2,1,0:T(8,128)(2,1)} %bitcast.88), calls=%async_computation.2 | async-start | bytes 8388608 | tf_op jit(solution)/shard_map/all_to_all | solution.py:140
  379.8 237.7 %all-gather.3.cloned.1.call-start = ((), (), s32[]{:S(2)}) async-start(), calls=%async_computation.4 | async-start | bytes 4718592 | tf_op jit(solution)/shard_map/all_gather | solution.py:146
  574.5 45.9 %copy-start.1 = (f32[128,2048]{1,0:T(8,128)S(1)}, f32[128,2048]{1,0:T(8,128)}, u32[]{:S(2)}) copy-start(f32[128,2048]{1,0:T(8,128)} %all-reduce.2.cloned.1.call-done) | copy-start | bytes 3145732
Sparse Core Ops, SparseCore 0:
  77.2 71.4 all-reduce.1
  575.8 41.6 all-gather.2
